TPU v7x, 128 devices: a whole 4x4x4 slice. The times are simulated.
128 devices in a mesh: region: 8 (over y, core), local: 16 (over z, x).
Axes of the slice: x: 4, y: 4, z: 4, core: 2. Of those that a mesh axis runs over, the one named last changes fastest.
Arguments:
- block_flags: int32 [32, 768], P(None, ('region', 'local')), may hold values 0 or 1
- trace: bfloat16 [32, 98304], P(None, ('region', 'local')), may hold values from 0.099609375 to 1
- w_region: bfloat16 [8, 12288, 12288], P('region', None, 'local'), may hold values from -0.0546875 to 0.0546875
- lr_weight: bfloat16 [8, 16, 8, 8, 128, 128], P('region', 'local'), may hold values from -0.1875 to 0.1875
- lr_source: int32 [8, 16, 8, 8], P('region', 'local'), may hold values from 0 to 5
- lr_target: int32 [8, 16, 8, 8], P('region', 'local'), may hold values from 0 to 95
- lr_count: int32 [8, 16, 8], P('region', 'local'), may hold values from 0 to 8, as said below
- g_decay: float32 [98304], P(('region', 'local')), may hold values from 0.5 to 0.97
- v_decay: float32 [98304], P(('region', 'local')), may hold values from 0.4 to 0.95
- g_start: float32 [98304], P(('region', 'local')), may hold values from -6 to 6
- v_start: float32 [98304], P(('region', 'local')), may hold values from -6 to 6
Outputs:
- membrane: float32 [32, 98304], P(None, ('region', 'local'))
- g_final: float32 [98304], P(('region', 'local'))
Inputs may be any that keep to these rules, and one draw needn't show every extreme that they name: lr_count is 0 for a region's own devices, exactly 8 from every device to the next region (d = (r + 1) % 8), and 1 to 8 otherwise.
All inputs are finite; a program needn't handle non-finite values. No bound on the sum of `block_flags` on one device may be relied on, other than what follows from the above.
Results may differ from a plain program's by a relative error of at most 0.0003.
Values may be sent and summed in bfloat16 or wider, within the bound.
A program may use at most 128 MiB of HBM per device.

v0:
```python
import jax
import jax.numpy as jnp
from jax import lax
from jax.sharding import PartitionSpec as P


def local(
    block_flags,
    trace,
    w_region,
    lr_weight,
    lr_source,
    lr_target,
    lr_count,
    g_decay,
    v_decay,
    g_start,
    v_start,
):
    steps = trace.shape[0]
    own_blocks = block_flags.shape[1]
    width = trace.shape[1] // own_blocks
    drive = (
        trace.reshape(steps, own_blocks, width) * block_flags[:, :, None].astype(jnp.bfloat16)
    ).reshape(steps, own_blocks * width)
    weights = w_region[0]
    rows = weights
    inner = jnp.dot(
        lax.all_gather(drive, "local", axis=1, tiled=True), rows, preferred_element_type=jnp.float32
    )
    counts = lr_count[0, 0]
    targets = lr_target[0, 0]
    sources = lr_source[0, 0]
    tiles = lr_weight[0, 0]
    regions = targets.shape[0]
    slots = targets.shape[1]
    blocks = drive.reshape(steps, own_blocks, width)
    chosen = jnp.take(blocks, sources, axis=1)
    partial_value = jnp.einsum("sdci,dcio->dcso", chosen, tiles, preferred_element_type=jnp.float32)
    live = (jnp.arange(slots, dtype=jnp.int32)[None, :] < counts[:, None]).astype(jnp.float32)
    partial_value = partial_value * live[:, :, None, None]
    arrived, arrived_ids = (
        lax.all_to_all(partial_value, "region", split_axis=0, concat_axis=0, tiled=True),
        lax.all_to_all(targets, "region", split_axis=0, concat_axis=0, tiled=True),
    )
    flat = arrived.reshape(regions * slots, steps * width)
    id_flat = arrived_ids.reshape(regions * slots)
    rows = jnp.arange(lax.axis_size("local") * own_blocks, dtype=jnp.int32)
    onehot = (id_flat[None, :] == rows[:, None]).astype(jnp.float32)
    outer = lax.psum_scatter(
        jnp.dot(onehot, flat, precision=lax.Precision.HIGHEST, preferred_element_type=jnp.float32),
        "local",
        scatter_dimension=0,
        tiled=True,
    )
    outer = (
        outer.reshape(own_blocks, steps, width)
        .transpose(1, 0, 2)
        .reshape(steps, own_blocks * width)
    )
    current = inner + outer

    def advance(carry, now):
        g_state, v_state = carry
        g_state = g_decay * g_state + (1.0 - g_decay) * now
        v_state = v_decay * v_state + (1.0 - v_decay) * g_state
        return ((g_state, v_state), v_state)

    (g_last, v_last), membrane = lax.scan(advance, (g_start, v_start), current)
    return (membrane, g_last)


def solution(mesh):
    return jax.shard_map(
        local,
        mesh=mesh,
        in_specs=(
            P(None, ("region", "local")),
            P(None, ("region", "local")),
            P("region", None, "local"),
            P("region", "local", None, None, None, None),
            P("region", "local", None, None),
            P("region", "local", None, None),
            P("region", "local", None),
            P(("region", "local")),
            P(("region", "local")),
            P(("region", "local")),
            P(("region", "local")),
        ),
        out_specs=(P(None, ("region", "local")), P(("region", "local"))),
        check_vma=False,
    )
```

profile of v0, /device:TPU:0, one launch (start us, length us, event | category | flops | bytes accessed | tf_op | source)
XLA Modules:
  0.0 195.3 jit_solution(16240093048172563462)
XLA Ops:
  7.2 0.0 copy-start
  7.2 4.7 %all-to-all-start = ((s32[8,1,8]{2,1,0:T(1,128)}), s32[8,1,8]{2,1,0:T(1,128)S(1)}, u32[]{:S(2)}, u32[]{:S(2)}) async-start(s32[8,1,8]{2,1,0:T(1,128)} %bitcast.50), calls=%async_computation | async-start | bytes 8192 | tf_op jit(solution)/shard_map/all_to_all | solution.py:44
  11.9 0.7 convert_element_type.12
  12.6 0.7 compare_select_fusion
  13.3 0.1 reshape.90
  13.3 0.8 fusion.18
  14.1 0.9 bitcast_multiply_fusion.1
  15.0 0.7 gather_fusion
  15.7 1.7 fusion.4
  17.4 0.0 all-to-all-done
  17.4 4.8 %all-to-all-start.1 = ((f32[8,8,32,128]{3,2,1,0:T(8,128)}), f32[8,8,32,128]{3,2,1,0:T(8,128)S(1)}, u32[]{:S(2)}, u32[]{:S(2)}) async-start(f32[8,8,32,128]{3,2,1,0:T(8,128)} %fusion.4), calls=%async_computation.1 | async-start | bytes 2097152 | tf_op jit(solution)/shard_map/all_to_all | solution.py:43
  22.2 0.0 all-reduce.3.cloned.1.call-start
  22.2 0.5 broadcast.63
  22.7 0.7 reduce.5
  23.4 0.1 eq.15
  23.5 14.7 %all-to-all-done.1 = f32[8,8,32,128]{3,2,1,0:T(8,128)S(1)} async-done(((f32[8,8,32,128]{3,2,1,0:T(8,128)}), f32[8,8,32,128]{3,2,1,0:T(8,128)S(1)}, u32[]{:S(2)}, u32[]{:S(2)}) %all-to-all-start.1) | async-done | bytes 1048608 | tf_op jit(solution)/shard_map/all_to_all | solution.py:43
  38.1 2.6 %fusion.10 = f32[96,4096]{1,0:T(8,128)} fusion(f32[8,8,32,128]{3,2,1,0:T(8,128)S(1)} %all-to-all-done.1, s32[64]{0:T(128)S(1)} %eq.15), kind=kOutput, calls=%fused_computation.10 | convolution fusion | flops 301996032 | bytes 2621696 | tf_op jit(solution)/shard_map/dot_general | solution.py:51
  40.7 0.0 all-reduce.3.cloned.1.call-update
  40.8 0.1 copy.23
  40.9 0.6 dynamic-slice
  42.1 0.1 mul.33.clone
  42.3 27.9 %all_gather.3 = bf16[32,12288]{1,0:T(8,128)(2,1)S(1)} all-gather(bf16[32,768]{1,0:T(8,128)(2,1)S(1)} %bitcast_multiply_fusion), channel_id=1, replica_groups=mesh['region'=8,'local'=16] {'local'}, dimensions={1}, use_global_device_ids=true | all-gather | bytes 835584 | tf_op jit(solution)/shard_map/all_gather | solution.py:29
  70.2 61.4 %all-reduce.3.cloned.1.call-done = f32[96,4096]{1,0:T(8,128)} async-done(((f32[96,4096]{1,0:T(8,128)}), f32[96,4096]{1,0:T(8,128)}) %all-reduce.3.cloned.1.call-update) | async-done | bytes 1572880
  131.6 1.0 constant_dynamic-slice_fusion
  132.6 0.0 copy-start.1
  132.6 0.0 copy-start.4
  132.6 0.0 copy-start.5
  132.6 0.0 copy-start.6
  132.6 9.6 %fusion.7 = f32[32,768]{1,0:T(8,128)S(1)} fusion(bf16[32,12288]{1,0:T(8,128)(2,1)S(1)} %all_gather.3, bf16[1,12288,768]{2,1,0:T(8,128)(2,1)} %param.15, f32[4,8,6,128]{3,2,1,0:T(8,128)S(1)} %bitcast.48), kind=kOutput, calls=%fused_computation.9 | convolution fusion | flops 604004352 | bytes 19857408 | tf_op jit(solution)/shard_map/dot_general | solution.py:28
  142.3 0.0 copy-done.1
  142.3 45.5 %while.14 = (s32[]{:T(128)}, f32[768]{0:T(1024)S(1)}, f32[768]{0:T(1024)S(1)}, f32[32,768]{1,0:T(8,128)}, f32[768]{0:T(1024)S(1)}, /*index=5*/f32[32,768]{1,0:T(8,128)S(1)}, f32[768]{0:T(1024)S(1)}, s32[]{:T(128)}, s32[]{:T(128)}) while((s32[]{:T(128)}, f32[768]{0:T(1024)S(1)}, f32[768]{0:T(1024)S(1)}, f32[32,768]{1,0:T(8,128)}, ...), condition=%wide.region_2.3_spmd, body=%wide.region_1.2_spmd.sunk | while | flops 6146 | bytes 40037 | solution.py:69
  142.4 1.4 dynamic_update_slice.5
  143.8 1.4 dynamic_update_slice.5
  145.2 1.4 dynamic_update_slice.5
  146.7 1.4 dynamic_update_slice.5
  148.1 1.4 dynamic_update_slice.5
  149.5 1.4 dynamic_update_slice.5
  150.9 1.4 dynamic_update_slice.5
  152.4 1.4 dynamic_update_slice.5
  153.8 1.4 dynamic_update_slice.5
  155.2 1.4 dynamic_update_slice.5
  156.6 1.4 dynamic_update_slice.5
  158.0 1.4 dynamic_update_slice.5
  159.5 1.4 dynamic_update_slice.5
  160.9 1.4 dynamic_update_slice.5
  162.3 1.4 dynamic_update_slice.5
  163.7 1.4 dynamic_update_slice.5
  165.2 1.4 dynamic_update_slice.5
  166.6 1.4 dynamic_update_slice.5
  168.0 1.4 dynamic_update_slice.5
  169.4 1.4 dynamic_update_slice.5
  170.8 1.4 dynamic_update_slice.5
  172.3 1.4 dynamic_update_slice.5
  173.7 1.4 dynamic_update_slice.5
  175.1 1.4 dynamic_update_slice.5
  176.5 1.4 dynamic_update_slice.5
  178.0 1.4 dynamic_update_slice.5
  179.4 1.4 dynamic_update_slice.5
  180.8 1.4 dynamic_update_slice.5
  182.2 1.4 dynamic_update_slice.5
  183.6 1.4 dynamic_update_slice.5
  185.1 1.4 dynamic_update_slice.5
  186.5 1.4 dynamic_update_slice.5
  187.9 0.6 copy-done.3
  (108 shorter events, 1.1 us)
Async XLA Ops:
  7.2 8.5 %copy-start = (bf16[1,1,8,8,128,128]{5,4,3,2,1,0:T(8,128)(2,1)S(1)}, bf16[1,1,8,8,128,128]{5,4,3,2,1,0:T(8,128)(2,1)}, u32[]{:S(2)}) copy-start(bf16[1,1,8,8,128,128]{5,4,3,2,1,0:T(8,128)(2,1)} %param.16) | copy-start | bytes 6291460
  7.2 10.2 %all-to-all-start = ((s32[8,1,8]{2,1,0:T(1,128)}), s32[8,1,8]{2,1,0:T(1,128)S(1)}, u32[]{:S(2)}, u32[]{:S(2)}) async-start(s32[8,1,8]{2,1,0:T(1,128)} %bitcast.50), calls=%async_computation | async-start | bytes 8192 | tf_op jit(solution)/shard_map/all_to_all | solution.py:44
  17.4 20.8 %all-to-all-start.1 = ((f32[8,8,32,128]{3,2,1,0:T(8,128)}), f32[8,8,32,128]{3,2,1,0:T(8,128)S(1)}, u32[]{:S(2)}, u32[]{:S(2)}) async-start(f32[8,8,32,128]{3,2,1,0:T(8,128)} %fusion.4), calls=%async_computation.1 | async-start | bytes 2097152 | tf_op jit(solution)/shard_map/all_to_all | solution.py:43
  22.2 109.5 %all-reduce.3.cloned.1.call-start = ((), (), s32[]{:S(2)}) async-start(), calls=%async_computation.2 | async-start | bytes 3145728
  23.5 17.4 %copy-start.7 = (u32[128]{0:T(128)S(1)}, u32[128]{0:T(128)}, u32[]{:S(2)}) copy-start(u32[128]{0:T(128)} %constant.38) | copy-start | bytes 1540
  23.5 18.8 %copy-start.2 = (bf16[32,768]{1,0:T(8,128)(2,1)S(1)}, bf16[32,768]{1,0:T(8,128)(2,1)}, u32[]{:S(2)}) copy-start(bf16[32,768]{1,0:T(8,128)(2,1)} %param.14) | copy-start | bytes 147460
  132.6 9.7 %copy-start.1 = (f32[768]{0:T(1024)S(1)}, f32[768]{0:T(1024)}, u32[]{:S(2)}) copy-start(f32[768]{0:T(1024)} %param.23) | copy-start | bytes 9220
  132.6 9.7 %copy-start.4 = (f32[768]{0:T(1024)S(1)}, f32[768]{0:T(1024)}, u32[]{:S(2)}) copy-start(f32[768]{0:T(1024)} %param.22) | copy-start | bytes 9220
  132.6 9.7 %copy-start.5 = (f32[768]{0:T(1024)S(1)}, f32[768]{0:T(1024)}, u32[]{:S(2)}) copy-start(f32[768]{0:T(1024)} %param.20) | copy-start | bytes 9220
  132.6 9.7 %copy-start.6 = (f32[768]{0:T(1024)S(1)}, f32[768]{0:T(1024)}, u32[]{:S(2)}) copy-start(f32[768]{0:T(1024)} %param.21) | copy-start | bytes 9220
  187.9 0.6 copy-start.3
Sparse Core Ops, SparseCore 0:
  40.9 90.7 all-reduce.2
where the time goes:
time: 198 us; the launch traced here: 195 us
  waiting for transfers between devices  76.1 us (38%)
  local copies, waits for them, and re-layouts  48.4 us (24%)
  blocking collectives  27.9 us (14%)
  between operations  14.8 us (7%)
  matrix products  13.9 us (7%)
  starting transfers between devices  9.54 us (5%)
  other arithmetic  4.04 us (2%)
    unnamed x2, waiting for transfers between devices  61.4 us
    dynamic_update_slice x32, local copies, waits for them, and re-layouts, local(): (g_last, v_last), membrane = lax.scan(advance, (g_start, v_start), current)  43.8 us
    all_gather x1, blocking collectives, local(): lax.all_gather(drive, 'local', axis=1, tiled=True)  27.9 us
    all_to_all x1, waiting for transfers between devices, local(): lax.all_to_all(partial_value, 'region', split_axis=0, concat_axis=0, tile...  14.7 us
    dot_general x1, matrix products, local(): jnp.dot(lax.all_gather(drive, 'local', axis=1, tiled=True), rows, preferr...  9.64 us
    all_to_all x1, starting transfers between devices, local(): lax.all_to_all(partial_value, 'region', split_axis=0, concat_axis=0, tile...  4.81 us
    all_to_all x1, starting transfers between devices, local(): lax.all_to_all(targets, 'region', split_axis=0, concat_axis=0, tiled=True)  4.7 us
  transfers between devices with their start and end apart: 3, of which 2 were waited for; matrix products, arithmetic and copies ran while one was open for 4% of the time, Pallas kernels for 0%

commit v1 on v0

--- a/solution.py
+++ b/solution.py
@@ -2,6 +2,22 @@
 import jax.numpy as jnp
 from jax import lax
 from jax.sharding import PartitionSpec as P
+
+
+def swapped_with_each(x, axis, split, join):
+    ways, here = (lax.axis_size(axis), lax.axis_index(axis))
+    width = x.shape[split] // ways
+    shape = list(x.shape)
+    shape[split] = width
+    height = shape[join]
+    shape[join] = height * ways
+    full = jnp.zeros(shape, x.dtype)
+    for mask in range(ways):
+        part = lax.dynamic_slice_in_dim(x, (here ^ mask) * width, width, axis=split)
+        if mask:
+            part = lax.ppermute(part, axis, [(d, d ^ mask) for d in range(ways)])
+        full = lax.dynamic_update_slice_in_dim(full, part, (here ^ mask) * height, axis=join)
+    return full
 
 
 def local(
@@ -41,7 +57,7 @@
     partial_value = partial_value * live[:, :, None, None]
     arrived, arrived_ids = (
         lax.all_to_all(partial_value, "region", split_axis=0, concat_axis=0, tiled=True),
-        lax.all_to_all(targets, "region", split_axis=0, concat_axis=0, tiled=True),
+        swapped_with_each(targets, "region", 0, 0),
     )
     flat = arrived.reshape(regions * slots, steps * width)
     id_flat = arrived_ids.reshape(regions * slots)

time: 198 us -> 197 us (level)
  starting transfers between devices: 9.54 us -> 14.3 us
  waiting for transfers between devices: 76.1 us -> 71.8 us
    all_to_all x1, waiting for transfers between devices: 14.7 us -> 0.01 us  [local(): lax.all_to_all(partial_value, 'region', split_axis=0, concat_axis=0, tile...]
    ppermute x0 -> x7, starting transfers between devices: none -> 9.75 us  [swapped_with_each(): part = lax.ppermute(part, axis, [(d, d ^ mask) for d in range(ways)])]
    ppermute x0 -> x7, waiting for transfers between devices: none -> 8.53 us  [swapped_with_each(): part = lax.ppermute(part, axis, [(d, d ^ mask) for d in range(ways)])]
    all_to_all x1 -> x0, starting transfers between devices: 4.7 us -> none  [local(): lax.all_to_all(targets, 'region', split_axis=0, concat_axis=0, tiled=True)]
  transfers between devices with their start and end apart: 3 -> 9, of which waited for: 2 -> 4; matrix products, arithmetic and copies ran while one was open for 4% -> 1% of each run, Pallas kernels for 0% -> 0%
where the time goes in v1:
time: 197 us; the launch traced here: 194 us
  waiting for transfers between devices  71.8 us (36%)
  local copies, waits for them, and re-layouts  48.1 us (24%)
  blocking collectives  27.4 us (14%)
  between operations  14.8 us (8%)
  starting transfers between devices  14.3 us (7%)
  matrix products  13.9 us (7%)
  other arithmetic  3.53 us (2%)
    unnamed x2, waiting for transfers between devices  63.2 us
    dynamic_update_slice x32, local copies, waits for them, and re-layouts, local(): (g_last, v_last), membrane = lax.scan(advance, (g_start, v_start), current)  43.8 us
    all_gather x1, blocking collectives, local(): lax.all_gather(drive, 'local', axis=1, tiled=True)  27.4 us
    ppermute x7, starting transfers between devices, swapped_with_each(): part = lax.ppermute(part, axis, [(d, d ^ mask) for d in range(ways)])  9.75 us
    dot_general x1, matrix products, local(): jnp.dot(lax.all_gather(drive, 'local', axis=1, tiled=True), rows, preferr...  9.64 us
    ppermute x7, waiting for transfers between devices, swapped_with_each(): part = lax.ppermute(part, axis, [(d, d ^ mask) for d in range(ways)])  8.53 us
    all_to_all x1, starting transfers between devices, local(): lax.all_to_all(partial_value, 'region', split_axis=0, concat_axis=0, tile...  4.56 us
  transfers between devices with their start and end apart: 9, of which 4 were waited for; matrix products, arithmetic and copies ran while one was open for 1% of the time, Pallas kernels for 0%

profile of v1, /device:TPU:0, one launch (start us, length us, event | category | flops | bytes accessed | tf_op | source)
XLA Modules:
  0.0 194.5 jit_solution(17237342494453984370)
XLA Ops:
  7.2 0.0 copy-start
  7.2 0.8 convert_element_type.12
  8.0 0.7 compare_select_fusion
  8.7 0.1 reshape.94
  8.8 0.8 fusion.18
  9.6 0.9 bitcast_multiply_fusion.1
  10.5 0.7 gather_fusion
  11.1 1.7 fusion.4
  12.8 4.6 %all-to-all-start = ((f32[8,8,32,128]{3,2,1,0:T(8,128)}), f32[8,8,32,128]{3,2,1,0:T(8,128)S(1)}, u32[]{:S(2)}, u32[]{:S(2)}) async-start(f32[8,8,32,128]{3,2,1,0:T(8,128)} %fusion.4), calls=%async_computation | async-start | bytes 2097152 | tf_op jit(solution)/shard_map/all_to_all | solution.py:59
  17.4 0.0 all-reduce.3.cloned.1.call-start
  17.5 0.5 collective-permute-start
  18.0 1.7 collective-permute-start.1
  19.7 3.2 %collective-permute-start.3 = (s32[1,8]{1,0:T(1,128)S(1)}, s32[1,8]{1,0:T(1,128)S(1)}, u32[]{:S(2)}, u32[]{:S(2)}) collective-permute-start(s32[1,8]{1,0:T(1,128)S(1)} %get-tuple-element.60), channel_id=1, source_target_pairs={{0,64},{16,80},{32,96},{48,112},{64,0},{80,16},{96,32},{112,48},{1... | collective-permute-start | bytes 104 | tf_op jit(solution)/shard_map/ppermute | solution.py:18
  22.9 0.1 collective-permute-start.4
  23.1 3.0 %collective-permute-start.5 = (s32[1,8]{1,0:T(1,128)S(1)}, s32[1,8]{1,0:T(1,128)S(1)}, u32[]{:S(2)}, u32[]{:S(2)}) collective-permute-start(s32[1,8]{1,0:T(1,128)S(1)} %get-tuple-element.65), channel_id=1, source_target_pairs={{0,96},{16,112},{32,64},{48,80},{64,32},{80,48},{96,0},{112,16},{1... | collective-permute-start | bytes 104 | tf_op jit(solution)/shard_map/ppermute | solution.py:18
  26.1 5.8 %collective-permute-done.1 = s32[1,8]{1,0:T(1,128)S(1)} collective-permute-done((s32[1,8]{1,0:T(1,128)S(1)}, s32[1,8]{1,0:T(1,128)S(1)}, u32[]{:S(2)}, u32[]{:S(2)}) %collective-permute-start.1) | collective-permute-done | bytes 64 | tf_op jit(solution)/shard_map/ppermute | solution.py:18
  31.9 1.3 collective-permute-start.6
  33.2 0.2 collective-permute-done.3
  33.6 2.5 %collective-permute-done.6 = s32[1,8]{1,0:T(1,128)S(1)} collective-permute-done((s32[1,8]{1,0:T(1,128)S(1)}, s32[1,8]{1,0:T(1,128)S(1)}, u32[]{:S(2)}, u32[]{:S(2)}) %collective-permute-start.6) | collective-permute-done | bytes 64 | tf_op jit(solution)/shard_map/ppermute | solution.py:18
  36.1 0.1 eq.15
  36.2 2.6 %fusion.10 = f32[96,4096]{1,0:T(8,128)} fusion(f32[8,8,32,128]{3,2,1,0:T(8,128)S(1)} %all-to-all-done, s32[64]{0:T(128)S(1)} %eq.15), kind=kOutput, calls=%fused_computation.10 | convolution fusion | flops 301996032 | bytes 2621696 | tf_op jit(solution)/shard_map/dot_general | solution.py:67
  38.7 0.0 all-reduce.3.cloned.1.call-update
  38.8 0.1 copy.22
  38.9 0.6 dynamic-slice.8
  40.0 0.1 mul.33.clone
  40.2 27.4 %all_gather.3 = bf16[32,12288]{1,0:T(8,128)(2,1)S(1)} all-gather(bf16[32,768]{1,0:T(8,128)(2,1)S(1)} %bitcast_multiply_fusion), channel_id=1, replica_groups=mesh['region'=8,'local'=16] {'local'}, dimensions={1}, use_global_device_ids=true | all-gather | bytes 835584 | tf_op jit(solution)/shard_map/all_gather | solution.py:45
  67.6 63.2 %all-reduce.3.cloned.1.call-done = f32[96,4096]{1,0:T(8,128)} async-done(((f32[96,4096]{1,0:T(8,128)}), f32[96,4096]{1,0:T(8,128)}) %all-reduce.3.cloned.1.call-update) | async-done | bytes 1572880
  130.8 1.0 constant_dynamic-slice_fusion.8
  131.8 9.6 %fusion.7 = f32[32,768]{1,0:T(8,128)S(1)} fusion(bf16[32,12288]{1,0:T(8,128)(2,1)S(1)} %all_gather.3, bf16[1,12288,768]{2,1,0:T(8,128)(2,1)} %param.15, f32[4,8,6,128]{3,2,1,0:T(8,128)S(1)} %bitcast.61), kind=kOutput, calls=%fused_computation.9 | convolution fusion | flops 604004352 | bytes 19857408 | tf_op jit(solution)/shard_map/dot_general | solution.py:44
  141.4 0.0 copy-done.1
  141.5 45.5 %while.14 = (s32[]{:T(128)}, f32[768]{0:T(1024)S(1)}, f32[768]{0:T(1024)S(1)}, f32[32,768]{1,0:T(8,128)}, f32[768]{0:T(1024)S(1)}, /*index=5*/f32[32,768]{1,0:T(8,128)S(1)}, f32[768]{0:T(1024)S(1)}, s32[]{:T(128)}, s32[]{:T(128)}) while((s32[]{:T(128)}, f32[768]{0:T(1024)S(1)}, f32[768]{0:T(1024)S(1)}, f32[32,768]{1,0:T(8,128)}, ...), condition=%wide.region_2.3_spmd, body=%wide.region_1.2_spmd.sunk | while | flops 6146 | bytes 40037 | solution.py:85
  141.6 1.4 dynamic_update_slice.37
  143.0 1.4 dynamic_update_slice.37
  144.4 1.4 dynamic_update_slice.37
  145.8 1.4 dynamic_update_slice.37
  147.2 1.4 dynamic_update_slice.37
  148.7 1.4 dynamic_update_slice.37
  150.1 1.4 dynamic_update_slice.37
  151.5 1.4 dynamic_update_slice.37
  152.9 1.4 dynamic_update_slice.37
  154.4 1.4 dynamic_update_slice.37
  155.8 1.4 dynamic_update_slice.37
  157.2 1.4 dynamic_update_slice.37
  158.6 1.4 dynamic_update_slice.37
  160.0 1.4 dynamic_update_slice.37
  161.5 1.4 dynamic_update_slice.37
  162.9 1.4 dynamic_update_slice.37
  164.3 1.4 dynamic_update_slice.37
  165.7 1.4 dynamic_update_slice.37
  167.2 1.4 dynamic_update_slice.37
  168.6 1.4 dynamic_update_slice.37
  170.0 1.4 dynamic_update_slice.37
  171.4 1.4 dynamic_update_slice.37
  172.8 1.4 dynamic_update_slice.37
  174.3 1.4 dynamic_update_slice.37
  175.7 1.4 dynamic_update_slice.37
  177.1 1.4 dynamic_update_slice.37
  178.5 1.4 dynamic_update_slice.37
  180.0 1.4 dynamic_update_slice.37
  181.4 1.4 dynamic_update_slice.37
  182.8 1.4 dynamic_update_slice.37
  184.2 1.4 dynamic_update_slice.37
  185.6 1.4 dynamic_update_slice.37
  187.0 0.6 copy-done.3
  (130 shorter events, 1.4 us)
Async XLA Ops:
  7.2 4.0 %copy-start = (bf16[1,1,8,8,128,128]{5,4,3,2,1,0:T(8,128)(2,1)S(1)}, bf16[1,1,8,8,128,128]{5,4,3,2,1,0:T(8,128)(2,1)}, u32[]{:S(2)}) copy-start(bf16[1,1,8,8,128,128]{5,4,3,2,1,0:T(8,128)(2,1)} %param.16) | copy-start | bytes 6291460
  11.1 6.4 %copy-start.7 = (s32[1,1,8,8]{3,2,1,0:T(8,128)S(1)}, s32[1,1,8,8]{3,2,1,0:T(8,128)}, u32[]{:S(2)}) copy-start(s32[1,1,8,8]{3,2,1,0:T(8,128)} %param.18) | copy-start | bytes 772
  12.8 23.3 %all-to-all-start = ((f32[8,8,32,128]{3,2,1,0:T(8,128)}), f32[8,8,32,128]{3,2,1,0:T(8,128)S(1)}, u32[]{:S(2)}, u32[]{:S(2)}) async-start(f32[8,8,32,128]{3,2,1,0:T(8,128)} %fusion.4), calls=%async_computation | async-start | bytes 2097152 | tf_op jit(solution)/shard_map/all_to_all | solution.py:59
  17.4 113.4 %all-reduce.3.cloned.1.call-start = ((), (), s32[]{:S(2)}) async-start(), calls=%async_computation.1 | async-start | bytes 3145728
  17.5 5.5 %collective-permute-start = (s32[1,8]{1,0:T(1,128)S(1)}, s32[1,8]{1,0:T(1,128)S(1)}, u32[]{:S(2)}, u32[]{:S(2)}) collective-permute-start(s32[1,8]{1,0:T(1,128)S(1)} %get-tuple-element.63), channel_id=1, source_target_pairs={{0,16},{16,0},{32,48},{48,32},{64,80},{80,64},{96,112},{112,96},{1... | collective-permute-start | bytes 104 | tf_op jit(solution)/shard_map/ppermute | solution.py:18
  18.0 13.8 %collective-permute-start.1 = (s32[1,8]{1,0:T(1,128)S(1)}, s32[1,8]{1,0:T(1,128)S(1)}, u32[]{:S(2)}, u32[]{:S(2)}) collective-permute-start(s32[1,8]{1,0:T(1,128)S(1)} %get-tuple-element.62), channel_id=1, source_target_pairs={{0,32},{16,48},{32,0},{48,16},{64,96},{80,112},{96,64},{112,80},{1... | collective-permute-start | bytes 104 | tf_op jit(solution)/shard_map/ppermute | solution.py:18
  19.7 13.5 %collective-permute-start.2 = (s32[1,8]{1,0:T(1,128)S(1)}, s32[1,8]{1,0:T(1,128)S(1)}, u32[]{:S(2)}, u32[]{:S(2)}) collective-permute-start(s32[1,8]{1,0:T(1,128)S(1)} %get-tuple-element.61), channel_id=1, source_target_pairs={{0,48},{16,32},{32,16},{48,0},{64,112},{80,96},{96,80},{112,64},{1... | collective-permute-start | bytes 104 | tf_op jit(solution)/shard_map/ppermute | solution.py:18
  19.7 13.8 %collective-permute-start.3 = (s32[1,8]{1,0:T(1,128)S(1)}, s32[1,8]{1,0:T(1,128)S(1)}, u32[]{:S(2)}, u32[]{:S(2)}) collective-permute-start(s32[1,8]{1,0:T(1,128)S(1)} %get-tuple-element.60), channel_id=1, source_target_pairs={{0,64},{16,80},{32,96},{48,112},{64,0},{80,16},{96,32},{112,48},{1... | collective-permute-start | bytes 104 | tf_op jit(solution)/shard_map/ppermute | solution.py:18
  22.9 10.6 %collective-permute-start.4 = (s32[1,8]{1,0:T(1,128)S(1)}, s32[1,8]{1,0:T(1,128)S(1)}, u32[]{:S(2)}, u32[]{:S(2)}) collective-permute-start(s32[1,8]{1,0:T(1,128)S(1)} %get-tuple-element.59), channel_id=1, source_target_pairs={{0,80},{16,64},{32,112},{48,96},{64,16},{80,0},{96,48},{112,32},{1... | collective-permute-start | bytes 104 | tf_op jit(solution)/shard_map/ppermute | solution.py:18
  23.1 10.5 %collective-permute-start.5 = (s32[1,8]{1,0:T(1,128)S(1)}, s32[1,8]{1,0:T(1,128)S(1)}, u32[]{:S(2)}, u32[]{:S(2)}) collective-permute-start(s32[1,8]{1,0:T(1,128)S(1)} %get-tuple-element.65), channel_id=1, source_target_pairs={{0,96},{16,112},{32,64},{48,80},{64,32},{80,48},{96,0},{112,16},{1... | collective-permute-start | bytes 104 | tf_op jit(solution)/shard_map/ppermute | solution.py:18
  31.9 4.2 %collective-permute-start.6 = (s32[1,8]{1,0:T(1,128)S(1)}, s32[1,8]{1,0:T(1,128)S(1)}, u32[]{:S(2)}, u32[]{:S(2)}) collective-permute-start(s32[1,8]{1,0:T(1,128)S(1)} %get-tuple-element.58), channel_id=1, source_target_pairs={{0,112},{16,96},{32,80},{48,64},{64,48},{80,32},{96,16},{112,0},{1... | collective-permute-start | bytes 104 | tf_op jit(solution)/shard_map/ppermute | solution.py:18
  36.2 2.7 %copy-start.8 = (u32[128]{0:T(128)S(1)}, u32[128]{0:T(128)}, u32[]{:S(2)}) copy-start(u32[128]{0:T(128)} %constant.67) | copy-start | bytes 1540
  36.2 4.0 %copy-start.2 = (bf16[32,768]{1,0:T(8,128)(2,1)S(1)}, bf16[32,768]{1,0:T(8,128)(2,1)}, u32[]{:S(2)}) copy-start(bf16[32,768]{1,0:T(8,128)(2,1)} %param.14) | copy-start | bytes 147460
  131.8 9.7 %copy-start.1 = (f32[768]{0:T(1024)S(1)}, f32[768]{0:T(1024)}, u32[]{:S(2)}) copy-start(f32[768]{0:T(1024)} %param.23) | copy-start | bytes 9220
  131.8 9.7 %copy-start.4 = (f32[768]{0:T(1024)S(1)}, f32[768]{0:T(1024)}, u32[]{:S(2)}) copy-start(f32[768]{0:T(1024)} %param.22) | copy-start | bytes 9220
  131.8 9.7 %copy-start.5 = (f32[768]{0:T(1024)S(1)}, f32[768]{0:T(1024)}, u32[]{:S(2)}) copy-start(f32[768]{0:T(1024)} %param.20) | copy-start | bytes 9220
  131.8 9.7 %copy-start.6 = (f32[768]{0:T(1024)S(1)}, f32[768]{0:T(1024)}, u32[]{:S(2)}) copy-start(f32[768]{0:T(1024)} %param.21) | copy-start | bytes 9220
  187.0 0.6 copy-start.3
Sparse Core Ops, SparseCore 0:
  38.9 91.8 all-reduce.2
